TPU v7x, 32 devices: a whole 2x2x4 slice. The times are simulated.
32 devices in a mesh: dp: 4 (over z), section: 2 (over core), ctx: 4 (over y, x).
Axes of the slice: x: 2, y: 2, z: 4, core: 2. Of those that a mesh axis runs over, the one named last changes fastest.
Arguments:
- features: bfloat16 [2, 4096, 8192], P('section', 'ctx', 'dp'), may hold values from -6 to 6
- queries: bfloat16 [2, 4096, 8192], P('section', 'ctx', 'dp'), may hold values from -6 to 6
- keys: bfloat16 [2, 4096, 1024], P('section', 'ctx', 'dp'), may hold values from -6 to 6
- values: bfloat16 [2, 4096, 1024], P('section', 'ctx', 'dp'), may hold values from -6 to 6
- attn_out: bfloat16 [2, 4096, 8192], P('section', 'ctx', 'dp'), may hold values from -4 to 4
- out_grad: bfloat16 [2, 4096, 8192], P('section', 'ctx', 'dp'), may hold values from -6 to 6
- lse: float32 [2, 64, 4096], P('section', 'dp', 'ctx'), as said below
- doc_starts: int32 [2, 65], P('section'), may hold values from 0 to 4096, as said below
- key_blocks: int32 [2, 32, 17], P('section', 'ctx'), may hold values from -1 to 31, as said below
Outputs:
- query_grad: bfloat16 [2, 4096, 8192], P('section', 'ctx', 'dp')
- key_grad: bfloat16 [2, 4096, 1024], P('section', 'ctx', 'dp')
- value_grad: bfloat16 [2, 4096, 1024], P('section', 'ctx', 'dp')
- value_weight_grad: float32 [2, 8192, 1024], P('section', ('dp', 'ctx'))
Inputs may be any that keep to these rules, and one draw needn't show every extreme that they name: `doc_starts`: each row lists the first token of each document of one sequence, rising from 0; entries after the last document equal 4096. Every document has 64 to 2049 tokens, except the last, which the sequence's end may cut shorter; one of the first two documents of every sequence has exactly 2049 tokens. `key_blocks`: row b of a section (query block b of 128 tokens) lists in rising order the key blocks from the block holding the start of the document of block b's first token up to b itself, then -1 in the remaining entries. Every section has a row with all 17 entries used. `lse`: Non-negative.
All inputs are finite; a program needn't handle non-finite values.
Results may differ from a plain program's by a relative error of at most 0.0065.
Values may be sent and summed in bfloat16 or wider, within the bound.
A program may use at most 128 MiB of HBM per device.

v0:
```python
import jax
import jax.numpy as jnp
from jax import lax
from jax.sharding import PartitionSpec as P

QH = 64
KVH = 8
HD = 128


def shifted(array, axis, by):
    length = lax.axis_size(axis)
    pairs = [(i, i + by) for i in range(length) if 0 <= i + by < length]
    return lax.ppermute(array, axis, pairs)


def shifted_2(value, axis, steps):
    count = lax.axis_size(axis)
    pairs = [(source, (source + steps) % count) for source in range(count)]
    return lax.ppermute(value, axis, pairs)


def doc_index(starts, positions):
    return jnp.sum((starts[None, :] <= positions[:, None]).astype(jnp.int32), axis=1) - 1


def local(features, queries, keys, values, attn_out, out_grad, lse, doc_starts, key_blocks):
    tok_rows = queries.shape[1]
    blocks_here = tok_rows // 128
    group_size = QH // KVH
    kv_local = keys.shape[2] // HD
    score_scale = HD ** (-0.5)
    kv_width = keys.shape[2]
    shard_pos = lax.axis_index("ctx")
    own_keys = keys[0]
    own_values = values[0]
    near_keys = []
    near_values = []
    hop_keys, hop_values = (own_keys, own_values)
    for hop_step in range(2):
        hop_keys, hop_values = shifted((hop_keys, hop_values), "ctx", 1)
        near_keys.insert(0, hop_keys)
        near_values.insert(0, hop_values)
    window_keys = jnp.concatenate(near_keys + [own_keys], axis=0)
    window_values = jnp.concatenate(near_values + [own_values], axis=0)
    starts = doc_starts[0]
    query_pos = shard_pos * tok_rows + jnp.arange(tok_rows, dtype=jnp.int32)
    window_pos = (shard_pos - 2) * tok_rows + jnp.arange(3 * tok_rows, dtype=jnp.int32)
    query_docs = doc_index(starts, query_pos)
    window_docs = doc_index(starts, window_pos)
    first_block = (shard_pos - 2) * blocks_here
    query_rows = queries[0].reshape(tok_rows, kv_local, group_size, HD)
    grad_rows = out_grad[0].reshape(tok_rows, kv_local, group_size, HD)
    output_rows = attn_out[0].reshape(tok_rows, kv_local, group_size, HD)
    lse_rows = lse[0].reshape(kv_local, group_size, tok_rows)
    key_grid = window_keys.reshape(3 * tok_rows, kv_local, HD)
    value_grid = window_values.reshape(3 * tok_rows, kv_local, HD)
    key_acc = jnp.zeros((3 * tok_rows, kv_local, HD), jnp.float32)
    value_acc = jnp.zeros((3 * tok_rows, kv_local, HD), jnp.float32)
    query_parts = []
    for block_idx in range(blocks_here):
        row_start = block_idx * 128
        query_block = query_rows[row_start : row_start + 128]
        grad_block = grad_rows[row_start : row_start + 128]
        output_block = output_rows[row_start : row_start + 128]
        row_delta = jnp.einsum(
            "igrd,igrd->gri", grad_block.astype(jnp.float32), output_block.astype(jnp.float32)
        )
        block_lse = lse_rows[:, :, row_start : row_start + 128]
        block_docs = query_docs[row_start : row_start + 128]
        block_pos = query_pos[row_start : row_start + 128]
        listed = key_blocks[0, block_idx]
        used_count = jnp.sum((listed >= 0).astype(jnp.int32))

        def visit_tile(entry_idx, state_carry):
            grad_query, key_sum, value_sum = state_carry
            local_start = (listed[entry_idx] - first_block) * 128
            key_tile = lax.dynamic_slice_in_dim(key_grid, local_start, 128, 0)
            value_tile = lax.dynamic_slice_in_dim(value_grid, local_start, 128, 0)
            tile_docs = lax.dynamic_slice_in_dim(window_docs, local_start, 128, 0)
            tile_pos = lax.dynamic_slice_in_dim(window_pos, local_start, 128, 0)
            allowed = (block_docs[:, None] == tile_docs[None, :]) & (
                block_pos[:, None] >= tile_pos[None, :]
            )
            scores = (
                jnp.einsum(
                    "igrd,jgd->grij", query_block, key_tile, preferred_element_type=jnp.float32
                )
                * score_scale
            )
            prob_full = jnp.where(allowed, jnp.exp(scores - block_lse[..., None]), 0.0)
            dprobs = jnp.einsum(
                "igrd,jgd->grij", grad_block, value_tile, preferred_element_type=jnp.float32
            )
            dscores = (prob_full * (dprobs - row_delta[..., None]) * score_scale).astype(
                jnp.bfloat16
            )
            prob_half = prob_full.astype(jnp.bfloat16)
            grad_query = grad_query + jnp.einsum(
                "grij,jgd->igrd", dscores, key_tile, preferred_element_type=jnp.float32
            )
            key_part = jnp.einsum(
                "grij,igrd->jgd", dscores, query_block, preferred_element_type=jnp.float32
            )
            value_part = jnp.einsum(
                "grij,igrd->jgd", prob_half, grad_block, preferred_element_type=jnp.float32
            )
            key_sum = lax.dynamic_update_slice_in_dim(
                key_sum,
                lax.dynamic_slice_in_dim(key_sum, local_start, 128, 0) + key_part,
                local_start,
                0,
            )
            value_sum = lax.dynamic_update_slice_in_dim(
                value_sum,
                lax.dynamic_slice_in_dim(value_sum, local_start, 128, 0) + value_part,
                local_start,
                0,
            )
            return (grad_query, key_sum, value_sum)

        start_query = jnp.zeros((128, kv_local, group_size, HD), jnp.float32)
        grad_query, key_acc, value_acc = lax.fori_loop(
            0, used_count, visit_tile, (start_query, key_acc, value_acc)
        )
        query_parts.append(grad_query.reshape(128, kv_local * group_size * HD))
    grad_queries = jnp.concatenate(query_parts, axis=0).astype(jnp.bfloat16)
    key_flat = key_acc.reshape(3 * tok_rows, kv_width)
    value_flat = value_acc.reshape(3 * tok_rows, kv_width)
    own_key_sum = key_flat[:tok_rows]
    own_value_sum = value_flat[:tok_rows]
    for slot_index in (1, 2):
        back_keys, back_values = (
            shifted(own_key_sum.astype(jnp.bfloat16), "ctx", -1).astype(own_key_sum.dtype),
            shifted(own_value_sum.astype(jnp.bfloat16), "ctx", -1).astype(own_value_sum.dtype),
        )
        own_key_sum = back_keys + key_flat[slot_index * tok_rows : (slot_index + 1) * tok_rows]
        own_value_sum = (
            back_values + value_flat[slot_index * tok_rows : (slot_index + 1) * tok_rows]
        )
    sent_query, sent_key, sent_value = shifted_2(
        (grad_queries, own_key_sum.astype(jnp.bfloat16), own_value_sum.astype(jnp.bfloat16)),
        "section",
        -1,
    )
    value_all = lax.all_gather(sent_value, "dp", axis=1, tiled=True)
    feature_rows = features[0]
    total_tokens = tok_rows * lax.axis_size("ctx")
    weight_sum = lax.psum_scatter(
        lax.dot_general(
            feature_rows, value_all, (((0,), (0,)), ((), ())), preferred_element_type=jnp.float32
        ),
        "ctx",
        scatter_dimension=0,
        tiled=True,
    )
    weight_grad = weight_sum * total_tokens ** (-0.5)
    return (sent_query[None], sent_key[None], sent_value[None], weight_grad[None])


def solution(mesh):
    placed = (
        P("section", "ctx", "dp"),
        P("section", "ctx", "dp"),
        P("section", "ctx", "dp"),
        P("section", "ctx", "dp"),
        P("section", "ctx", "dp"),
        P("section", "ctx", "dp"),
        P("section", "dp", "ctx"),
        P("section", None),
        P("section", "ctx", None),
    )
    return jax.shard_map(
        local,
        mesh=mesh,
        in_specs=placed,
        out_specs=(
            P("section", "ctx", "dp"),
            P("section", "ctx", "dp"),
            P("section", "ctx", "dp"),
            P("section", ("dp", "ctx"), None),
        ),
        check_vma=False,
    )
```

profile of v0, /device:TPU:0, one launch (start us, length us, event | category | flops | bytes accessed | tf_op | source)
XLA Modules:
  0.0 1566.5 jit_solution(2956470902719302222)
XLA Ops:
  9.3 5.6 collective-permute-start
  17.0 3.4 collective-permute-start.2
  21.8 3.5 fusion.199
  27.0 4.2 slice_bitcast_fusion.4
  65.5 3.5 collective-permute-start.1
  124.6 2.6 pad_maximum_fusion
  129.8 2.6 pad_maximum_fusion.1
  139.9 13.5 while.112
  154.6 26.3 %while.113 = (s32[]{:T(128)}, f32[128,2,8,128]{0,3,2,1:T(8,128)}, f32[3072,2,128]{2,0,1:T(8,128)}, f32[3072,2,128]{2,0,1:T(8,128)}, s32[]{:T(128)}, /*index=5*/s...) while((s32[]{:T(128)}, f32[128,2,8,128]{0,3,2,1:T(8,128)}, ...), condition=%wide.region_7.8_spmd, body=%wide.region_6.7_spmd.sunk | while | flops 338018304 | bytes 13881729 | solution.py:123
  182.1 38.1 %while.114 = (s32[]{:T(128)}, f32[128,2,8,128]{0,3,2,1:T(8,128)}, f32[3072,2,128]{2,0,1:T(8,128)}, f32[3072,2,128]{2,0,1:T(8,128)}, s32[]{:T(128)}, /*index=5*/s...) while((s32[]{:T(128)}, f32[128,2,8,128]{0,3,2,1:T(8,128)}, ...), condition=%wide.region_10.11_spmd, body=%wide.region_9.10_spmd.sunk | while | flops 338018304 | bytes 11784549 | solution.py:123
  221.4 51.2 %while.115 = (s32[]{:T(128)}, f32[128,2,8,128]{0,3,2,1:T(8,128)}, f32[3072,2,128]{2,0,1:T(8,128)}, f32[3072,2,128]{2,0,1:T(8,128)}, s32[]{:T(128)}, /*index=5*/s...) while((s32[]{:T(128)}, f32[128,2,8,128]{0,3,2,1:T(8,128)}, ...), condition=%wide.region_13.14_spmd, body=%wide.region_12.13_spmd.sunk | while | flops 338018304 | bytes 11784549 | solution.py:123
  273.8 61.8 %while.116 = (s32[]{:T(128)}, f32[128,2,8,128]{0,3,2,1:T(8,128)}, f32[3072,2,128]{2,0,1:T(8,128)}, f32[3072,2,128]{2,0,1:T(8,128)}, s32[]{:T(128)}, /*index=5*/s...) while((s32[]{:T(128)}, f32[128,2,8,128]{0,3,2,1:T(8,128)}, ...), condition=%wide.region_16.17_spmd, body=%wide.region_15.16_spmd.sunk | while | flops 338018304 | bytes 9687369 | solution.py:123
  283.4 2.6 fusion.447
  295.7 2.6 fusion.447
  307.9 2.6 fusion.447
  320.1 2.6 fusion.447
  332.3 2.6 fusion.447
  336.8 73.4 %while.117 = (s32[]{:T(128)}, f32[128,2,8,128]{0,3,2,1:T(8,128)}, f32[3072,2,128]{2,0,1:T(8,128)}, f32[3072,2,128]{2,0,1:T(8,128)}, s32[]{:T(128)}, /*index=5*/s...) while((s32[]{:T(128)}, f32[128,2,8,128]{0,3,2,1:T(8,128)}, ...), condition=%wide.region_19.20_spmd, body=%wide.region_18.19_spmd.sunk | while | flops 338018304 | bytes 9687369 | solution.py:123
  358.5 2.6 fusion.462
  370.6 2.6 fusion.462
  382.7 2.6 fusion.462
  394.9 2.6 fusion.462
  410.4 76.8 %while.118 = (s32[]{:T(128)}, f32[128,2,8,128]{0,3,2,1:T(8,128)S(1)}, f32[3072,2,128]{2,0,1:T(8,128)}, f32[3072,2,128]{2,0,1:T(8,128)}, s32[]{:T(128)}, /*index=...) while((s32[]{:T(128)}, ...), condition=%wide.region_22.23_spmd, body=%wide.region_21.22_spmd.sunk | while | flops 338018304 | bytes 9687369 | solution.py:123
  488.3 87.8 %while.119 = (s32[]{:T(128)}, f32[128,2,8,128]{0,3,2,1:T(8,128)S(1)}, f32[3072,2,128]{2,0,1:T(8,128)}, f32[3072,2,128]{2,0,1:T(8,128)}, s32[]{:T(128)}, /*index=...) while((s32[]{:T(128)}, ...), condition=%wide.region_25.26_spmd, body=%wide.region_24.25_spmd.sunk | while | flops 338018304 | bytes 9687369 | solution.py:123
  580.4 785.0 %collective-permute-done.8 = bf16[1024,256]{1,0:T(8,128)(2,1)S(1)} collective-permute-done((bf16[1024,256]{1,0:T(8,128)(2,1)S(1)}, bf16[1024,256]{1,0:T(8,128)(2,1)S(1)}, u32[]{:S(2)}, u32[]{:S(2)}) %collective-permute-start.8) | collective-permute-done | bytes 524320 | tf_op jit(solution)/shard_map/ppermute | solution.py:14
  1366.8 13.7 collective-permute-done.9
  1383.7 47.5 %all-gather.2.cloned.1.call-done = bf16[1024,1024]{1,0:T(8,128)(2,1)} async-done(((bf16[1024,256]{1,0:T(8,128)(2,1)}), bf16[1024,1024]{1,0:T(8,128)(2,1)}) %all-gather.2.cloned.1.call-update) | async-done | bytes 2097168 | tf_op jit(solution)/shard_map/all_gather | solution.py:146
  1431.2 10.7 convolution_bitcast_fusion.32
  1461.5 26.1 %collective-permute-done.5 = bf16[1024,256]{1,0:T(8,128)(2,1)S(1)} collective-permute-done((bf16[1024,256]{1,0:T(8,128)(2,1)S(1)}, bf16[1024,256]{1,0:T(8,128)(2,1)S(1)}, u32[]{:S(2)}, u32[]{:S(2)}) %collective-permute-start.5) | collective-permute-done | bytes 524320 | tf_op jit(solution)/shard_map/ppermute | solution.py:14
  1489.0 26.6 %collective-permute-done.6 = bf16[1024,256]{1,0:T(8,128)(2,1)S(1)} collective-permute-done((bf16[1024,256]{1,0:T(8,128)(2,1)S(1)}, bf16[1024,256]{1,0:T(8,128)(2,1)S(1)}, u32[]{:S(2)}, u32[]{:S(2)}) %collective-permute-start.6) | collective-permute-done | bytes 524320 | tf_op jit(solution)/shard_map/ppermute | solution.py:14
  1517.7 31.4 %reduce-scatter.2.cloned.1.call-done = f32[512,1024]{0,1:T(8,128)} async-done(((f32[2048,1024]{0,1:T(8,128)}), f32[512,1024]{0,1:T(8,128)}) %reduce-scatter.2.cloned.1.call-update) | async-done | bytes 2097168 | tf_op jit(solution)/shard_map/reduce_scatter | solution.py:149
  1552.8 4.8 copy.496
  (615 shorter events, 502.2 us)
Async XLA Ops:
  7.2 1424.1 %all-gather.2.cloned.1.call-start = ((), (), s32[]{:S(2)}) async-start(), calls=%async_computation.1 | async-start | bytes 2621440 | tf_op jit(solution)/shard_map/all_gather | solution.py:146
  9.3 56.2 %collective-permute-start = (bf16[1024,256]{0,1:T(8,128)(2,1)}, bf16[1024,256]{0,1:T(8,128)(2,1)}, u32[]{:S(2)}, u32[]{:S(2)}) collective-permute-start(bf16[1024,256]{0,1:T(8,128)(2,1)} %bitcast.137), channel_id=1, source_target_pairs={{0,1},{1,2},{2,3},{4,5},{5,6},{6,7},{8,9},{9,10},{10,11},{12,13},{... | collective-permute-start | bytes 1572872 | tf_op jit(solution)/shard_map/ppermute | solution.py:14
  17.0 59.5 %collective-permute-start.2 = (bf16[1024,256]{0,1:T(8,128)(2,1)}, bf16[1024,256]{0,1:T(8,128)(2,1)}, u32[]{:S(2)}, u32[]{:S(2)}) collective-permute-start(bf16[1024,256]{0,1:T(8,128)(2,1)} %bitcast.144), channel_id=1, source_target_pairs={{0,1},{1,2},{2,3},{4,5},{5,6},{6,7},{8,9},{9,10},{10,11},{12,13},{... | collective-permute-start | bytes 1572872 | tf_op jit(solution)/shard_map/ppermute | solution.py:14
  65.5 59.1 %collective-permute-start.1 = (bf16[1024,256]{0,1:T(8,128)(2,1)}, bf16[1024,256]{0,1:T(8,128)(2,1)}, u32[]{:S(2)}, u32[]{:S(2)}) collective-permute-start(bf16[1024,256]{0,1:T(8,128)(2,1)} %collective-permute-done), channel_id=1, source_target_pairs={{0,1},{1,2},{2,3},{4,5},{5,6},{6,7},{8,9},{9,10},{10,11},{12,13},{... | collective-permute-start | bytes 1572872 | tf_op jit(solution)/shard_map/ppermute | solution.py:14
  76.4 53.4 %collective-permute-start.3 = (bf16[1024,256]{0,1:T(8,128)(2,1)}, bf16[1024,256]{0,1:T(8,128)(2,1)}, u32[]{:S(2)}, u32[]{:S(2)}) collective-permute-start(bf16[1024,256]{0,1:T(8,128)(2,1)} %collective-permute-done.2), channel_id=1, source_target_pairs={{0,1},{1,2},{2,3},{4,5},{5,6},{6,7},{8,9},{9,10},{10,11},{12,13},{... | collective-permute-start | bytes 1572872 | tf_op jit(solution)/shard_map/ppermute | solution.py:14
  221.3 52.4 %copy-start.5 = (bf16[128,2,8,128]{3,0,2,1:T(8,128)(2,1)S(1)}, bf16[128,2,8,128]{3,0,2,1:T(8,128)(2,1)}, u32[]{:S(2)}) copy-start(bf16[128,2,8,128]{3,0,2,1:T(8,128)(2,1)} %copy.180) | copy-start | bytes 1572868
  221.3 52.4 %copy-start.33 = (f32[2,8,128]{2,1,0:T(8,128)S(1)}, f32[2,8,128]{2,1,0:T(8,128)}, u32[]{:S(2)}) copy-start(f32[2,8,128]{2,1,0:T(8,128)} %get-tuple-element.2489) | copy-start | bytes 24580
  221.3 52.4 %copy-start.34 = (f32[2,8,128]{2,1,0:T(8,128)S(1)}, f32[2,8,128]{2,1,0:T(8,128)}, u32[]{:S(2)}) copy-start(f32[2,8,128]{2,1,0:T(8,128)} %copy.292) | copy-start | bytes 24580
  221.3 52.4 %copy-start.50 = (s32[128]{0:T(128)S(1)}, s32[128]{0:T(128)}, u32[]{:S(2)}) copy-start(s32[128]{0:T(128)} %get-tuple-element.2486) | copy-start | bytes 1540
  221.4 52.4 %copy-start.51 = (s32[128]{0:T(128)S(1)}, s32[128]{0:T(128)}, u32[]{:S(2)}) copy-start(s32[128]{0:T(128)} %get-tuple-element.2484) | copy-start | bytes 1540
  221.4 52.4 %copy-start.66 = (s32[17]{0:T(128)S(1)}, s32[17]{0:T(128)}, u32[]{:S(2)}) copy-start(s32[17]{0:T(128)} %get-tuple-element.2481) | copy-start | bytes 208
  273.8 63.0 %copy-start.4 = (bf16[128,2,8,128]{3,0,2,1:T(8,128)(2,1)S(1)}, bf16[128,2,8,128]{3,0,2,1:T(8,128)(2,1)}, u32[]{:S(2)}) copy-start(bf16[128,2,8,128]{3,0,2,1:T(8,128)(2,1)} %copy.187) | copy-start | bytes 1572868
  273.8 63.0 %copy-start.32 = (f32[2,8,128]{2,1,0:T(8,128)S(1)}, f32[2,8,128]{2,1,0:T(8,128)}, u32[]{:S(2)}) copy-start(f32[2,8,128]{2,1,0:T(8,128)} %get-tuple-element.2555) | copy-start | bytes 24580
  273.8 63.0 %copy-start.48 = (s32[128]{0:T(128)S(1)}, s32[128]{0:T(128)}, u32[]{:S(2)}) copy-start(s32[128]{0:T(128)} %get-tuple-element.2552) | copy-start | bytes 1540
  273.8 62.9 %copy-start.49 = (s32[128]{0:T(128)S(1)}, s32[128]{0:T(128)}, u32[]{:S(2)}) copy-start(s32[128]{0:T(128)} %get-tuple-element.2550) | copy-start | bytes 1540
  273.8 62.9 %copy-start.65 = (s32[17]{0:T(128)S(1)}, s32[17]{0:T(128)}, u32[]{:S(2)}) copy-start(s32[17]{0:T(128)} %get-tuple-element.2547) | copy-start | bytes 208
  336.8 73.6 %copy-start.3 = (bf16[128,2,8,128]{3,0,2,1:T(8,128)(2,1)S(1)}, bf16[128,2,8,128]{3,0,2,1:T(8,128)(2,1)}, u32[]{:S(2)}) copy-start(bf16[128,2,8,128]{3,0,2,1:T(8,128)(2,1)} %copy.194) | copy-start | bytes 1572868
  336.8 73.6 %copy-start.46 = (s32[128]{0:T(128)S(1)}, s32[128]{0:T(128)}, u32[]{:S(2)}) copy-start(s32[128]{0:T(128)} %get-tuple-element.2618) | copy-start | bytes 1540
  336.8 73.6 %copy-start.47 = (s32[128]{0:T(128)S(1)}, s32[128]{0:T(128)}, u32[]{:S(2)}) copy-start(s32[128]{0:T(128)} %get-tuple-element.2616) | copy-start | bytes 1540
  336.8 73.6 %copy-start.64 = (s32[17]{0:T(128)S(1)}, s32[17]{0:T(128)}, u32[]{:S(2)}) copy-start(s32[17]{0:T(128)} %get-tuple-element.2613) | copy-start | bytes 208
  410.4 77.9 %copy-start.2 = (bf16[128,2,8,128]{3,0,2,1:T(8,128)(2,1)S(1)}, bf16[128,2,8,128]{3,0,2,1:T(8,128)(2,1)}, u32[]{:S(2)}) copy-start(bf16[128,2,8,128]{3,0,2,1:T(8,128)(2,1)} %copy.201) | copy-start | bytes 1572868
  410.4 77.9 %copy-start.44 = (s32[128]{0:T(128)S(1)}, s32[128]{0:T(128)}, u32[]{:S(2)}) copy-start(s32[128]{0:T(128)} %get-tuple-element.2684) | copy-start | bytes 1540
  410.4 77.9 %copy-start.45 = (s32[128]{0:T(128)S(1)}, s32[128]{0:T(128)}, u32[]{:S(2)}) copy-start(s32[128]{0:T(128)} %get-tuple-element.2682) | copy-start | bytes 1540
  410.4 77.9 %copy-start.63 = (s32[17]{0:T(128)S(1)}, s32[17]{0:T(128)}, u32[]{:S(2)}) copy-start(s32[17]{0:T(128)} %get-tuple-element.2679) | copy-start | bytes 208
  577.4 787.9 %collective-permute-start.8 = (bf16[1024,256]{1,0:T(8,128)(2,1)S(1)}, bf16[1024,256]{1,0:T(8,128)(2,1)S(1)}, u32[]{:S(2)}, u32[]{:S(2)}) collective-permute-start(bf16[1024,256]{1,0:T(8,128)(2,1)S(1)} %copy_bitcast_fusion), channel_id=1, source_target_pairs={{1,0},{2,1},{3,2},{5,4},{6,5},{7,6},{9,8},{10,9},{11,10},{13,12},{... | collective-permute-start | bytes 1572872 | tf_op jit(solution)/shard_map/ppermute | solution.py:14
  1365.5 15.0 collective-permute-start.9
  1380.6 2.0 collective-permute-start.10
  1383.4 165.7 %reduce-scatter.2.cloned.1.call-start = ((), (), s32[]{:S(2)}) async-start(), calls=%async_computation.2 | async-start | bytes 10485760 | tf_op jit(solution)/shard_map/reduce_scatter | solution.py:149
  1459.1 58.6 %collective-permute-start.4 = (bf16[1024,2048]{1,0:T(8,128)(2,1)S(1)}, bf16[1024,2048]{1,0:T(8,128)(2,1)}, u32[]{:S(2)}, u32[]{:S(2)}) collective-permute-start(bf16[1024,2048]{1,0:T(8,128)(2,1)S(1)} %constant_dynamic-update-slice_fusion), channel_id=1, source_target_pairs={{0,4},{4,0},{1,5},{5,1},{2,6},{6,2},{3,7},{7,3},{8,12},{12,8},{9,1... | collective-permute-start | bytes 12582920 | tf_op jit(solution)/shard_map/ppermute | solution.py:20
  1460.0 27.5 %collective-permute-start.5 = (bf16[1024,256]{1,0:T(8,128)(2,1)S(1)}, bf16[1024,256]{1,0:T(8,128)(2,1)S(1)}, u32[]{:S(2)}, u32[]{:S(2)}) collective-permute-start(bf16[1024,256]{1,0:T(8,128)(2,1)S(1)} %copy_bitcast_fusion.1), channel_id=1, source_target_pairs={{1,0},{2,1},{3,2},{5,4},{6,5},{7,6},{9,8},{10,9},{11,10},{13,12},{... | collective-permute-start | bytes 1572872 | tf_op jit(solution)/shard_map/ppermute | solution.py:14
  1487.7 27.9 %collective-permute-start.6 = (bf16[1024,256]{1,0:T(8,128)(2,1)S(1)}, bf16[1024,256]{1,0:T(8,128)(2,1)S(1)}, u32[]{:S(2)}, u32[]{:S(2)}) collective-permute-start(bf16[1024,256]{1,0:T(8,128)(2,1)S(1)} %fusion.188), channel_id=1, source_target_pairs={{1,0},{2,1},{3,2},{5,4},{6,5},{7,6},{9,8},{10,9},{11,10},{13,12},{... | collective-permute-start | bytes 1572872 | tf_op jit(solution)/shard_map/ppermute | solution.py:14
  1515.7 2.0 collective-permute-start.7
  (59 other events, 695.6 us)
Sparse Core Ops, SparseCore 0:
  1383.5 47.6 all-gather.1
  1442.1 107.0 reduce-scatter.1
where the time goes:
time: 1560 us; the launch traced here: 1570 us
  waiting for transfers between devices  934 us (60%)
  matrix products  306 us (20%)
  local copies, waits for them, and re-layouts  203 us (13%)
  loops' own time  53.8 us (3%)
  other arithmetic  32.7 us (2%)
  starting transfers between devices  20.5 us (1%)
    ppermute x8, waiting for transfers between devices, shifted(): return lax.ppermute(array, axis, pairs)  851 us
    dot_general x36, matrix products, visit_tile(): jnp.einsum('grij,jgd->igrd', dscores, key_tile, preferred_element_type=jn...  74.2 us
    unnamed x178, local copies, waits for them, and re-layouts  69.9 us
    dot_general x36, matrix products, visit_tile(): jnp.einsum('grij,igrd->jgd', dscores, query_block, preferred_element_type...  67 us
    dot_general x36, matrix products, visit_tile(): jnp.einsum('grij,igrd->jgd', prob_half, grad_block, preferred_element_typ...  66.4 us
    another operation x8, loops' own time, local(): lax.fori_loop(0, used_count, visit_tile, (start_query, key_acc, value_acc))  53.8 us
    all_gather x1, waiting for transfers between devices, local(): value_all = lax.all_gather(sent_value, 'dp', axis=1, tiled=True)  47.5 us
    dot_general x36, matrix products, visit_tile(): jnp.einsum('igrd,jgd->grij', query_block, key_tile, preferred_element_typ...  44 us
  transfers between devices with their start and end apart: 13, of which 8 were waited for; matrix products, arithmetic and copies ran while one was open for 8% of the time, Pallas kernels for 0%

commit v1 on v0

v1 whole, which is shorter than its diff:
```python
import functools

import jax
import jax.numpy as jnp
from jax import lax
from jax.experimental import pallas as pl
from jax.experimental.pallas import tpu as pltpu
from jax.sharding import PartitionSpec as P

QH = 64
KVH = 8
HD = 128
GROUP = QH // KVH
LOG2E = 1.4426950408889634
KT = 256
ROWS = 256
CHUNKS = GROUP * 128 // ROWS


def attn_kernel(bounds, q_ref, do_ref, lse_ref, delta_ref, beg_ref, k0, k1, k2, v0, v1, v2,
                dq_ref, dk_ref, dv_ref, kbuf, vbuf, dkacc, dvacc, qs, dos, dqacc):
    step = pl.program_id(0)
    tok = k0.shape[0]
    base = 2 * tok
    scale = HD ** -0.5

    @pl.when(step == 0)
    def _():
        for slot, (kr, vr) in enumerate(((k0, v0), (k1, v1), (k2, v2))):
            kbuf[slot * tok:(slot + 1) * tok, :] = kr[...]
            vbuf[slot * tok:(slot + 1) * tok, :] = vr[...]
        dkacc[...] = jnp.zeros_like(dkacc)
        dvacc[...] = jnp.zeros_like(dvacc)

    for h in range(GROUP):
        qs[h * 128:(h + 1) * 128, :] = q_ref[:, h * HD:(h + 1) * HD]
        dos[h * 128:(h + 1) * 128, :] = do_ref[:, h * HD:(h + 1) * HD]
    dqacc[...] = jnp.zeros_like(dqacc)

    lo = bounds[0, step]
    mid = bounds[1, step]
    last = bounds[2, step]
    row0 = base + step * 128

    def tile(pair, masked):
        start = pl.multiple_of(pair * KT, KT)
        k = kbuf[pl.ds(start, KT), :]
        v = vbuf[pl.ds(start, KT), :]
        if masked:
            u = lax.broadcasted_iota(jnp.int32, (KT, ROWS), 0) + start
            t = (lax.broadcasted_iota(jnp.int32, (1, ROWS), 1) & 127) + row0
            allowed = (u >= beg_ref[0]) & (u <= t)
        dk = None
        dv = None
        for c in range(CHUNKS):
            at = slice(c * ROWS, (c + 1) * ROWS)
            q = qs[at, :]
            g = dos[at, :]
            s = lax.dot_general(k, q, (((1,), (1,)), ((), ())), preferred_element_type=jnp.float32)
            p = jnp.exp2(s * (scale * LOG2E) - lse_ref[0, 0, c:c + 1, :])
            if masked:
                p = jnp.where(allowed, p, 0.0)
            dp = lax.dot_general(v, g, (((1,), (1,)), ((), ())), preferred_element_type=jnp.float32)
            ds = (p * (dp - delta_ref[0, 0, c:c + 1, :])).astype(jnp.bfloat16)
            pb = p.astype(jnp.bfloat16)
            dvc = jnp.dot(pb, g, preferred_element_type=jnp.float32)
            dkc = jnp.dot(ds, q, preferred_element_type=jnp.float32)
            dk = dkc if dk is None else dk + dkc
            dv = dvc if dv is None else dv + dvc
            dqacc[at, :] += lax.dot_general(ds, k, (((0,), (0,)), ((), ())), preferred_element_type=jnp.float32)
        dkacc[pl.ds(start, KT), :] += dk
        dvacc[pl.ds(start, KT), :] += dv

    edge = mid - lo

    def masked_step(i, carry):
        tile(jnp.where(i < edge, lo + i, last), True)
        return carry

    def plain_step(i, carry):
        tile(i, False)
        return carry

    lax.fori_loop(0, edge + 1, masked_step, 0)
    lax.fori_loop(mid, last, plain_step, 0)

    for h in range(GROUP):
        dq_ref[:, h * HD:(h + 1) * HD] = (dqacc[h * 128:(h + 1) * 128, :] * scale).astype(jnp.bfloat16)

    @pl.when(step == pl.num_programs(0) - 1)
    def _():
        for slot in range(3):
            dk_ref[slot] = (dkacc[slot * tok:(slot + 1) * tok, :] * scale).astype(jnp.bfloat16)
            dv_ref[slot] = dvacc[slot * tok:(slot + 1) * tok, :].astype(jnp.bfloat16)


def attention(head, bounds, q, do, lse, delta, beg, ks, vs):
    tok = q.shape[0]
    blocks = tok // 128
    width = GROUP * HD
    spec_q = pl.BlockSpec((128, width), lambda i, *_: (i, head))
    spec_row = pl.BlockSpec((1, 1, CHUNKS, ROWS), lambda i, *_: (head, i, 0, 0))
    spec_kv = pl.BlockSpec((tok, HD), lambda i, *_: (0, head))
    spec_grad = pl.BlockSpec((3, tok, HD), lambda i, *_: (0, 0, 0))
    pairs = blocks * 11 // 2
    return pl.pallas_call(
        attn_kernel,
        out_shape=(
            jax.ShapeDtypeStruct((tok, width), jnp.bfloat16),
            jax.ShapeDtypeStruct((3, tok, HD), jnp.bfloat16),
            jax.ShapeDtypeStruct((3, tok, HD), jnp.bfloat16),
        ),
        grid_spec=pltpu.PrefetchScalarGridSpec(
            num_scalar_prefetch=1,
            grid=(blocks,),
            in_specs=[spec_q, spec_q, spec_row, spec_row,
                      pl.BlockSpec((1, 1, ROWS), lambda i, *_: (i, 0, 0))] + [spec_kv] * 6,
            out_specs=[pl.BlockSpec((128, width), lambda i, *_: (i, 0)), spec_grad, spec_grad],
            scratch_shapes=[
                pltpu.VMEM((3 * tok, HD), jnp.bfloat16),
                pltpu.VMEM((3 * tok, HD), jnp.bfloat16),
                pltpu.VMEM((3 * tok, HD), jnp.float32),
                pltpu.VMEM((3 * tok, HD), jnp.float32),
                pltpu.VMEM((width, HD), jnp.bfloat16),
                pltpu.VMEM((width, HD), jnp.bfloat16),
                pltpu.VMEM((width, HD), jnp.float32),
            ],
        ),
        compiler_params=pltpu.CompilerParams(
            dimension_semantics=("arbitrary",), vmem_limit_bytes=40 << 20),
        cost_estimate=pl.CostEstimate(
            flops=pairs * 10 * KT * width * HD, transcendentals=pairs * KT * width,
            bytes_accessed=10 << 20),
        name="attn_grad",
    )(bounds, q, do, lse, delta, beg, *ks, *vs)


def block_tables(starts, shard, tok):
    blocks = tok // 128
    pos = shard * tok + jnp.arange(tok, dtype=jnp.int32)
    begin = jnp.max(jnp.where(starts[None, :] <= pos[:, None], starts[None, :], 0), axis=1)
    begin = (begin - (shard - 2) * tok).reshape(blocks, 128)
    last = (2 * tok // 128 + jnp.arange(blocks, dtype=jnp.int32)) * 128 // KT
    lo = begin[:, 0] // KT
    mid = jnp.minimum((begin[:, -1] + KT - 1) // KT, last)
    beg = jnp.tile(begin, (1, ROWS // 128)).reshape(blocks, 1, ROWS)
    return jnp.stack([lo, mid, last]).astype(jnp.int32), beg


def row_tables(array, kv_local):
    blocks = array.shape[1] // 128
    grid = array.reshape(kv_local, CHUNKS, ROWS // 128, blocks, 128)
    return jnp.transpose(grid, (0, 3, 1, 2, 4)).reshape(kv_local, blocks, CHUNKS, ROWS)


def ctx_send(array, by):
    n = lax.axis_size("ctx")
    return lax.ppermute(array, "ctx", [(i, i + by) for i in range(n) if 0 <= i + by < n])


def home(array, by):
    n = lax.axis_size("ctx")
    m = lax.axis_size("section")
    pairs = [(s * n + i, (s - 1) % m * n + i - by)
             for s in range(m) for i in range(n) if i - by >= 0]
    return lax.ppermute(array, ("section", "ctx"), pairs)


def local(features, queries, keys, values, attn_out, out_grad, lse, doc_starts, key_blocks):
    tok = queries.shape[1]
    kv_local = keys.shape[2] // HD
    shard = lax.axis_index("ctx")
    ctx = lax.axis_size("ctx")
    dp = lax.axis_size("dp")
    own_k, own_v = keys[0], values[0]
    k1, v1 = ctx_send((own_k, own_v), 1)
    k0, v0 = ctx_send((own_k, own_v), 2)
    bounds, beg = block_tables(doc_starts[0], shard, tok)
    delta = jnp.einsum(
        "igd,igd->gi",
        out_grad[0].astype(jnp.float32).reshape(tok, kv_local * GROUP, HD),
        attn_out[0].astype(jnp.float32).reshape(tok, kv_local * GROUP, HD))
    delta = row_tables(delta, kv_local)
    lse2 = row_tables(lse[0] * LOG2E, kv_local)
    feat = features[0]
    scale = (tok * ctx) ** -0.5
    rows = feat.shape[1] // ctx
    dq_parts, dk_parts, dv_parts, w_parts = [], [], [], []
    for head in range(kv_local):
        dq, dk, dv = attention(head, bounds, queries[0], out_grad[0], lse2, delta, beg,
                               (k0, k1, own_k), (v0, v1, own_v))
        dv_sum = home(dv[2], 0).astype(jnp.float32) + home(dv[1], 1) + home(dv[0], 2)
        dv_sum = dv_sum.astype(jnp.bfloat16)
        dv_all = lax.all_gather(dv_sum, "dp", axis=1, tiled=True)
        dk_sum = home(dk[2], 0).astype(jnp.float32) + home(dk[1], 1) + home(dk[0], 2)
        dq_parts.append(home(dq, 0))
        dk_parts.append(dk_sum.astype(jnp.bfloat16))
        dv_parts.append(dv_sum)

        def partial(target):
            cols = lax.dynamic_slice_in_dim(feat, target * rows, rows, 1)
            return lax.dot_general(cols, dv_all, (((0,), (0,)), ((), ())),
                                   preferred_element_type=jnp.float32)

        total = partial(shard)
        for by in range(1, ctx):
            sent = partial((shard + by) % ctx).astype(jnp.bfloat16)
            total = total + lax.ppermute(sent, "ctx", [(i, (i + by) % ctx) for i in range(ctx)])
        w_parts.append((total * scale).reshape(rows, dp, 1, HD))
    weight = jnp.concatenate(w_parts, axis=2).reshape(rows, dp * kv_local * HD)
    return (jnp.concatenate(dq_parts, axis=1)[None],
            jnp.concatenate(dk_parts, axis=1)[None],
            jnp.concatenate(dv_parts, axis=1)[None],
            weight[None])


def solution(mesh):
    placed = (
        P("section", "ctx", "dp"),
        P("section", "ctx", "dp"),
        P("section", "ctx", "dp"),
        P("section", "ctx", "dp"),
        P("section", "ctx", "dp"),
        P("section", "ctx", "dp"),
        P("section", "dp", "ctx"),
        P("section", None),
        P("section", "ctx", None),
    )
    return jax.shard_map(
        local,
        mesh=mesh,
        in_specs=placed,
        out_specs=(
            P("section", "ctx", "dp"),
            P("section", "ctx", "dp"),
            P("section", "ctx", "dp"),
            P("section", ("dp", "ctx"), None),
        ),
        check_vma=False,
    )
```

time: 1560 us -> 337 us (0.22)
  waiting for transfers between devices: 934 us -> 159 us
  matrix products: 306 us -> 15.6 us
  local copies, waits for them, and re-layouts: 203 us -> 29.6 us
  Pallas kernels: 0 us -> 63.5 us
  loops' own time: 53.8 us -> 0 us
  other arithmetic: 32.7 us -> 14.4 us
    ppermute x11 -> x24, waiting for transfers between devices: 855 us -> 157 us  [the longest x14 107 us: home(): return lax.ppermute(array, ('section', 'ctx'), pairs)]
    dot_general x181 -> x8, matrix products: 306 us -> 15.6 us  [partial(): lax.dot_general(cols, dv_all, (((0,), (0,)), ((), ())), preferred_element...]
    dynamic_slice x108 -> x0, local copies, waits for them, and re-layouts: 75.7 us -> none  [the longest x36 27.7 us: visit_tile(): tile_pos = lax.dynamic_slice_in_dim(window_pos, local_start, 128, 0)]
    pallas_call x0 -> x2, Pallas kernels: none -> 63.5 us  [attention(): pl.pallas_call(attn_kernel, out_shape=(jax.ShapeDtypeStruct((tok, width),...]
    another operation x8 -> x0, loops' own time: 53.8 us -> none  [local(): lax.fori_loop(0, used_count, visit_tile, (start_query, key_acc, value_acc))]
    unnamed x178 -> x42, local copies, waits for them, and re-layouts: 69.9 us -> 20.8 us
    all_gather x1 -> x2, waiting for transfers between devices: 47.5 us -> 1.95 us  [local(): dv_all = lax.all_gather(dv_sum, 'dp', axis=1, tiled=True)]
    reduce_scatter x1 -> x0, waiting for transfers between devices: 31.4 us -> none  [local(): lax.psum_scatter(lax.dot_general(feature_rows, value_all, (((0,), (0,)),...]
  transfers between devices with their start and end apart: 13 -> 26, of which waited for: 8 -> 14; matrix products, arithmetic and copies ran while one was open for 8% -> 11% of each run, Pallas kernels for 0% -> 10%
where the time goes in v1:
time: 337 us; the launch traced here: 332 us
  waiting for transfers between devices  159 us (47%)
  Pallas kernels  63.5 us (19%)
  starting transfers between devices  35.5 us (11%)
  local copies, waits for them, and re-layouts  29.6 us (9%)
  matrix products  15.6 us (5%)
  between operations  14.6 us (4%)
  other arithmetic  14.4 us (4%)
    ppermute x14, waiting for transfers between devices, home(): return lax.ppermute(array, ('section', 'ctx'), pairs)  107 us
    pallas_call x2, Pallas kernels, attention(): pl.pallas_call(attn_kernel, out_shape=(jax.ShapeDtypeStruct((tok, width),...  63.5 us
    ppermute x4, waiting for transfers between devices, ctx_send(): lax.ppermute(array, 'ctx', [(i, i + by) for i in range(n) if 0 <= i + by...  26.3 us
    ppermute x6, waiting for transfers between devices, local(): lax.ppermute(sent, 'ctx', [(i, (i + by) % ctx) for i in range(ctx)])  23.3 us
    unnamed x42, local copies, waits for them, and re-layouts  20.8 us
    dot_general x8, matrix products, partial(): lax.dot_general(cols, dv_all, (((0,), (0,)), ((), ())), preferred_element...  15.6 us
    ppermute x14, starting transfers between devices, home(): return lax.ppermute(array, ('section', 'ctx'), pairs)  11.9 us
    ppermute x6, starting transfers between devices, local(): lax.ppermute(sent, 'ctx', [(i, (i + by) % ctx) for i in range(ctx)])  11.8 us
  transfers between devices with their start and end apart: 26, of which 14 were waited for; matrix products, arithmetic and copies ran while one was open for 11% of the time, Pallas kernels for 10%

profile of v1, /device:TPU:0, one launch (start us, length us, event | category | flops | bytes accessed | tf_op | source)
XLA Modules:
  0.0 331.5 jit_solution(7388017454535266060)
XLA Ops:
  7.2 4.9 %collective-permute-start.1 = (bf16[1024,256]{1,0:T(8,128)(2,1)}, bf16[1024,256]{1,0:T(8,128)(2,1)S(1)}, u32[]{:S(2)}, u32[]{:S(2)}) collective-permute-start(bf16[1024,256]{1,0:T(8,128)(2,1)} %bitcast.106), channel_id=1, source_target_pairs={{0,1},{1,2},{2,3},{4,5},{5,6},{6,7},{8,9},{9,10},{10,11},{12,13},{... | collective-permute-start | bytes 1572872 | tf_op jit(solution)/shard_map/ppermute | solution.py:158
  12.1 3.4 %collective-permute-start = (bf16[1024,256]{1,0:T(8,128)(2,1)}, bf16[1024,256]{1,0:T(8,128)(2,1)S(1)}, u32[]{:S(2)}, u32[]{:S(2)}) collective-permute-start(bf16[1024,256]{1,0:T(8,128)(2,1)} %bitcast.107), channel_id=1, source_target_pairs={{0,2},{1,3},{4,6},{5,7},{8,10},{9,11},{12,14},{13,15},{16,18},{17,... | collective-permute-start | bytes 1572872 | tf_op jit(solution)/shard_map/ppermute | solution.py:158
  16.9 1.9 collective-permute-start.2
  20.7 3.7 %copy.60 = bf16[128,8,16,128]{3,2,1,0:T(8,128)(2,1)S(1)} copy(bf16[128,8,16,128]{3,1,2,0:T(8,128)(2,1)} %bitcast.116) | data formatting | bytes 8388608
  25.9 3.1 fusion
  30.3 16.7 %collective-permute-done.k0 = bf16[1024,256]{1,0:T(8,128)(2,1)S(1)} collective-permute-done((bf16[1024,256]{1,0:T(8,128)(2,1)}, bf16[1024,256]{1,0:T(8,128)(2,1)S(1)}, u32[]{:S(2)}, u32[]{:S(2)}) %collective-permute-start) | collective-permute-done | bytes 524320 | tf_op jit(solution)/shard_map/ppermute | solution.py:158
  48.6 9.6 %collective-permute-done.2.v0 = bf16[1024,256]{1,0:T(8,128)(2,1)S(1)} collective-permute-done((bf16[1024,256]{1,0:T(8,128)(2,1)}, bf16[1024,256]{1,0:T(8,128)(2,1)S(1)}, u32[]{:S(2)}, u32[]{:S(2)}) %collective-permute-start.2) | collective-permute-done | bytes 524320 | tf_op jit(solution)/shard_map/ppermute | solution.py:158
  59.0 2.2 copy-done
  64.3 31.8 %attn_grad.3 = (bf16[1024,1024]{1,0:T(8,128)(2,1)S(1)}, bf16[3,1024,128]{2,1,0:T(8,128)(2,1)S(1)}, bf16[3,1024,128]{2,1,0:T(8,128)(2,1)S(1)}) custom-call(s32[3,8]{1,0:T(4,128)S(1)} %pad_add_fusion.bounds, bf16[1024,2048]{1,0:T(8,128)(2,1)S(1)} %bitcast.104, bf16[1024,2048]{1,0:T(8,128)(2,1)} %bitcast.117, f32[2,8,4,256]{3,2,1,0:T(4,128)S(1)} %reshape.243.lse_ref, ...), custom_call_target="tpu_custom_call" | custom-call | flops 14763950080 | bytes 10485760 | tf_op jit(solution)/shard_map/attn_grad/pallas_call | solution.py:106
  100.1 40.2 %collective-permute-done.17 = bf16[1024,128]{1,0:T(8,128)(2,1)S(1)} collective-permute-done((bf16[1024,128]{1,0:T(8,128)(2,1)S(1)}, bf16[1024,128]{1,0:T(8,128)(2,1)S(1)}, u32[]{:S(2)}, u32[]{:S(2)}) %collective-permute-start.17) | collective-permute-done | bytes 262176 | tf_op jit(solution)/shard_map/ppermute | solution.py:166
  141.4 2.2 copy-done.1
  146.7 31.7 %attn_grad.2 = (bf16[1024,1024]{1,0:T(8,128)(2,1)S(1)}, bf16[3,1024,128]{2,1,0:T(8,128)(2,1)S(1)}, bf16[3,1024,128]{2,1,0:T(8,128)(2,1)S(1)}) custom-call(s32[3,8]{1,0:T(4,128)S(1)} %pad_add_fusion.bounds, bf16[1024,2048]{1,0:T(8,128)(2,1)S(1)} %bitcast.105, bf16[1024,2048]{1,0:T(8,128)(2,1)} %bitcast.118, f32[2,8,4,256]{3,2,1,0:T(4,128)S(1)} %reshape.243.lse_ref, ...), custom_call_target="tpu_custom_call" | custom-call | flops 14763950080 | bytes 10485760 | tf_op jit(solution)/shard_map/attn_grad/pallas_call | solution.py:106
  186.6 38.4 %collective-permute-done.14 = bf16[1024,128]{1,0:T(8,128)(2,1)S(1)} collective-permute-done((bf16[1024,128]{1,0:T(8,128)(2,1)S(1)}, bf16[1024,128]{1,0:T(8,128)(2,1)S(1)}, u32[]{:S(2)}, u32[]{:S(2)}) %collective-permute-start.14) | collective-permute-done | bytes 262176 | tf_op jit(solution)/shard_map/ppermute | solution.py:166
  225.0 12.3 %collective-permute-done.13 = bf16[1024,128]{1,0:T(8,128)(2,1)S(1)} collective-permute-done((bf16[1024,128]{1,0:T(8,128)(2,1)S(1)}, bf16[1024,128]{1,0:T(8,128)(2,1)S(1)}, u32[]{:S(2)}, u32[]{:S(2)}) %collective-permute-start.13) | collective-permute-done | bytes 262176 | tf_op jit(solution)/shard_map/ppermute | solution.py:166
  243.1 1.8 maximum_bitcast_fusion.2
  244.9 4.1 %collective-permute-done.8 = bf16[1024,128]{1,0:T(8,128)(2,1)S(1)} collective-permute-done((bf16[1024,128]{1,0:T(8,128)(2,1)S(1)}, bf16[1024,128]{1,0:T(8,128)(2,1)S(1)}, u32[]{:S(2)}, u32[]{:S(2)}) %collective-permute-start.8) | collective-permute-done | bytes 262176 | tf_op jit(solution)/shard_map/ppermute | solution.py:166
  249.0 10.8 %collective-permute-done.7 = bf16[1024,128]{1,0:T(8,128)(2,1)S(1)} collective-permute-done((bf16[1024,128]{1,0:T(8,128)(2,1)S(1)}, bf16[1024,128]{1,0:T(8,128)(2,1)S(1)}, u32[]{:S(2)}, u32[]{:S(2)}) %collective-permute-start.7) | collective-permute-done | bytes 262176 | tf_op jit(solution)/shard_map/ppermute | solution.py:166
  260.7 3.2 convolution_convert_fusion.2
  263.9 6.8 %collective-permute-start.21 = (bf16[512,512]{0,1:T(8,128)(2,1)}, bf16[512,512]{0,1:T(8,128)(2,1)S(1)}, u32[]{:S(2)}, u32[]{:S(2)}) collective-permute-start(bf16[512,512]{0,1:T(8,128)(2,1)} %convolution_convert_fusion.2), channel_id=1, source_target_pairs={{0,1},{1,2},{2,3},{3,0},{4,5},{5,6},{6,7},{7,4},{8,9},{9,10},{10,1... | collective-permute-start | bytes 1572872 | tf_op jit(solution)/shard_map/ppermute | solution.py:208
  270.8 2.3 convolution_convert_fusion.1
  273.2 2.8 convolution_convert_fusion
  276.0 1.4 collective-permute-start.23
  277.4 2.0 all-gather.3.cloned.1.call-done
  279.4 2.4 convolution_convert_fusion.3
  281.8 2.3 convolution_convert_fusion.4
  285.5 1.5 collective-permute-start.19
  286.9 1.5 collective-permute-start.20
  288.4 4.8 %maximum_bitcast_fusion = bf16[1,1024,2048]{2,1,0:T(8,128)(2,1)} fusion(bf16[1024,1024]{1,0:T(8,128)(2,1)} %collective-permute-done.5, bf16[1024,1024]{1,0:T(8,128)(2,1)} %collective-permute-done.4), kind=kLoop, calls=%fused_computation.2 | loop fusion | flops 8388608 | bytes 8388608 | tf_op jit(solution)/shard_map/broadcast_in_dim | solution.py:211
  295.9 9.8 %collective-permute-done.18 = bf16[512,512]{0,1:T(8,128)(2,1)S(1)} collective-permute-done((bf16[512,512]{0,1:T(8,128)(2,1)S(1)}, bf16[512,512]{0,1:T(8,128)(2,1)S(1)}, u32[]{:S(2)}, u32[]{:S(2)}) %collective-permute-start.18) | collective-permute-done | bytes 524320 | tf_op jit(solution)/shard_map/ppermute | solution.py:208
  305.7 10.5 %collective-permute-done.19 = bf16[512,512]{0,1:T(8,128)(2,1)S(1)} collective-permute-done((bf16[512,512]{0,1:T(8,128)(2,1)S(1)}, bf16[512,512]{0,1:T(8,128)(2,1)S(1)}, u32[]{:S(2)}, u32[]{:S(2)}) %collective-permute-start.19) | collective-permute-done | bytes 524320 | tf_op jit(solution)/shard_map/ppermute | solution.py:208
  318.3 2.5 copy.44
  320.8 3.9 %broadcast_in_dim_reshape.3 = f32[1,512,1024]{2,1,0:T(8,128)} reshape(f32[512,4,2,128]{3,2,1,0:T(2,128)} %copy.44) | data formatting | bytes 4194304 | tf_op jit(solution)/shard_map/broadcast_in_dim;reshape | solution.py:214
  (101 shorter events, 40.7 us)
Async XLA Ops:
  7.2 253.6 %all-gather.5.cloned.1.call-start = ((), (), s32[]{:S(2)}) async-start(), calls=%async_computation.1 | async-start | bytes 1310720 | tf_op jit(solution)/shard_map/all_gather | solution.py:194
  7.2 23.1 %collective-permute-start.1 = (bf16[1024,256]{1,0:T(8,128)(2,1)}, bf16[1024,256]{1,0:T(8,128)(2,1)S(1)}, u32[]{:S(2)}, u32[]{:S(2)}) collective-permute-start(bf16[1024,256]{1,0:T(8,128)(2,1)} %bitcast.106), channel_id=1, source_target_pairs={{0,1},{1,2},{2,3},{4,5},{5,6},{6,7},{8,9},{9,10},{10,11},{12,13},{... | collective-permute-start | bytes 1572872 | tf_op jit(solution)/shard_map/ppermute | solution.py:158
  12.1 34.9 %collective-permute-start = (bf16[1024,256]{1,0:T(8,128)(2,1)}, bf16[1024,256]{1,0:T(8,128)(2,1)S(1)}, u32[]{:S(2)}, u32[]{:S(2)}) collective-permute-start(bf16[1024,256]{1,0:T(8,128)(2,1)} %bitcast.107), channel_id=1, source_target_pairs={{0,2},{1,3},{4,6},{5,7},{8,10},{9,11},{12,14},{13,15},{16,18},{17,... | collective-permute-start | bytes 1572872 | tf_op jit(solution)/shard_map/ppermute | solution.py:158
  15.5 32.3 %collective-permute-start.3 = (bf16[1024,256]{1,0:T(8,128)(2,1)}, bf16[1024,256]{1,0:T(8,128)(2,1)S(1)}, u32[]{:S(2)}, u32[]{:S(2)}) collective-permute-start(bf16[1024,256]{1,0:T(8,128)(2,1)} %bitcast.110), channel_id=1, source_target_pairs={{0,1},{1,2},{2,3},{4,5},{5,6},{6,7},{8,9},{9,10},{10,11},{12,13},{... | collective-permute-start | bytes 1572872 | tf_op jit(solution)/shard_map/ppermute | solution.py:158
  16.9 41.3 %collective-permute-start.2 = (bf16[1024,256]{1,0:T(8,128)(2,1)}, bf16[1024,256]{1,0:T(8,128)(2,1)S(1)}, u32[]{:S(2)}, u32[]{:S(2)}) collective-permute-start(bf16[1024,256]{1,0:T(8,128)(2,1)} %bitcast.111), channel_id=1, source_target_pairs={{0,2},{1,3},{4,6},{5,7},{8,10},{9,11},{12,14},{13,15},{16,18},{17,... | collective-permute-start | bytes 1572872 | tf_op jit(solution)/shard_map/ppermute | solution.py:158
  25.9 33.1 %copy-start.4 = (bf16[1,1024,256]{2,1,0:T(8,128)(2,1)S(1)}, bf16[1,1024,256]{2,1,0:T(8,128)(2,1)}, u32[]{:S(2)}) copy-start(bf16[1,1024,256]{2,1,0:T(8,128)(2,1)} %param.11) | copy-start | bytes 1572868
  25.9 33.1 %copy-start.5 = (bf16[1,1024,256]{2,1,0:T(8,128)(2,1)S(1)}, bf16[1,1024,256]{2,1,0:T(8,128)(2,1)}, u32[]{:S(2)}) copy-start(bf16[1,1024,256]{2,1,0:T(8,128)(2,1)} %param.12) | copy-start | bytes 1572868
  97.4 2.7 collective-permute-start.15
  97.5 42.8 %collective-permute-start.17 = (bf16[1024,128]{1,0:T(8,128)(2,1)S(1)}, bf16[1024,128]{1,0:T(8,128)(2,1)S(1)}, u32[]{:S(2)}, u32[]{:S(2)}) collective-permute-start(bf16[1024,128]{1,0:T(8,128)(2,1)S(1)} %get-tuple-element.22), channel_id=1, source_target_pairs={{2,4},{3,5},{6,0},{7,1},{10,12},{11,13},{14,8},{15,9},{18,20},{19,... | collective-permute-start | bytes 786440 | tf_op jit(solution)/shard_map/ppermute | solution.py:166
  98.8 41.5 %collective-permute-start.16 = (bf16[1024,128]{1,0:T(8,128)(2,1)S(1)}, bf16[1024,128]{1,0:T(8,128)(2,1)S(1)}, u32[]{:S(2)}, u32[]{:S(2)}) collective-permute-start(bf16[1024,128]{1,0:T(8,128)(2,1)S(1)} %get-tuple-element.23), channel_id=1, source_target_pairs={{1,4},{2,5},{3,6},{5,0},{6,1},{7,2},{9,12},{10,13},{11,14},{13,8},... | collective-permute-start | bytes 786440 | tf_op jit(solution)/shard_map/ppermute | solution.py:166
  141.2 138.2 %all-gather.3.cloned.1.call-start = ((), (), s32[]{:S(2)}) async-start(), calls=%async_computation | async-start | bytes 1310720 | tf_op jit(solution)/shard_map/all_gather | solution.py:194
  179.8 63.2 %copy-start.16 = (bf16[1024,128]{1,0:T(8,128)(2,1)S(1)}, bf16[1024,128]{1,0:T(8,128)(2,1)}, u32[]{:S(2)}) copy-start(bf16[1024,128]{1,0:T(8,128)(2,1)} %add_convert_fusion) | copy-start | bytes 786436
  179.9 5.4 %collective-permute-start.12 = (bf16[1024,128]{1,0:T(8,128)(2,1)S(1)}, bf16[1024,128]{1,0:T(8,128)(2,1)S(1)}, u32[]{:S(2)}, u32[]{:S(2)}) collective-permute-start(bf16[1024,128]{1,0:T(8,128)(2,1)S(1)} %get-tuple-element.18), channel_id=1, source_target_pairs={{0,4},{1,5},{2,6},{3,7},{4,0},{5,1},{6,2},{7,3},{8,12},{9,13},{10,... | collective-permute-start | bytes 786440 | tf_op jit(solution)/shard_map/ppermute | solution.py:166
  180.0 45.0 %collective-permute-start.14 = (bf16[1024,128]{1,0:T(8,128)(2,1)S(1)}, bf16[1024,128]{1,0:T(8,128)(2,1)S(1)}, u32[]{:S(2)}, u32[]{:S(2)}) collective-permute-start(bf16[1024,128]{1,0:T(8,128)(2,1)S(1)} %get-tuple-element.19), channel_id=1, source_target_pairs={{2,4},{3,5},{6,0},{7,1},{10,12},{11,13},{14,8},{15,9},{18,20},{19,... | collective-permute-start | bytes 786440 | tf_op jit(solution)/shard_map/ppermute | solution.py:166
  181.3 56.0 %collective-permute-start.13 = (bf16[1024,128]{1,0:T(8,128)(2,1)S(1)}, bf16[1024,128]{1,0:T(8,128)(2,1)S(1)}, u32[]{:S(2)}, u32[]{:S(2)}) collective-permute-start(bf16[1024,128]{1,0:T(8,128)(2,1)S(1)} %get-tuple-element.20), channel_id=1, source_target_pairs={{1,4},{2,5},{3,6},{5,0},{6,1},{7,2},{9,12},{10,13},{11,14},{13,8},... | collective-permute-start | bytes 786440 | tf_op jit(solution)/shard_map/ppermute | solution.py:166
  183.5 56.5 %collective-permute-start.9 = (bf16[1024,128]{1,0:T(8,128)(2,1)}, bf16[1024,128]{1,0:T(8,128)(2,1)S(1)}, u32[]{:S(2)}, u32[]{:S(2)}) collective-permute-start(bf16[1024,128]{1,0:T(8,128)(2,1)} %get-tuple-element.27), channel_id=1, source_target_pairs={{0,4},{1,5},{2,6},{3,7},{4,0},{5,1},{6,2},{7,3},{8,12},{9,13},{10,... | collective-permute-start | bytes 786440 | tf_op jit(solution)/shard_map/ppermute | solution.py:166
  184.0 57.3 %collective-permute-start.11 = (bf16[1024,128]{1,0:T(8,128)(2,1)}, bf16[1024,128]{1,0:T(8,128)(2,1)S(1)}, u32[]{:S(2)}, u32[]{:S(2)}) collective-permute-start(bf16[1024,128]{1,0:T(8,128)(2,1)} %get-tuple-element.28), channel_id=1, source_target_pairs={{2,4},{3,5},{6,0},{7,1},{10,12},{11,13},{14,8},{15,9},{18,20},{19,... | collective-permute-start | bytes 786440 | tf_op jit(solution)/shard_map/ppermute | solution.py:166
  185.3 57.5 %collective-permute-start.10 = (bf16[1024,128]{1,0:T(8,128)(2,1)}, bf16[1024,128]{1,0:T(8,128)(2,1)S(1)}, u32[]{:S(2)}, u32[]{:S(2)}) collective-permute-start(bf16[1024,128]{1,0:T(8,128)(2,1)} %get-tuple-element.29), channel_id=1, source_target_pairs={{1,4},{2,5},{3,6},{5,0},{6,1},{7,2},{9,12},{10,13},{11,14},{13,8},... | collective-permute-start | bytes 786440 | tf_op jit(solution)/shard_map/ppermute | solution.py:166
  238.1 6.8 %collective-permute-start.6 = (bf16[1024,128]{1,0:T(8,128)(2,1)S(1)}, bf16[1024,128]{1,0:T(8,128)(2,1)S(1)}, u32[]{:S(2)}, u32[]{:S(2)}) collective-permute-start(bf16[1024,128]{1,0:T(8,128)(2,1)S(1)} %get-tuple-element.24), channel_id=1, source_target_pairs={{0,4},{1,5},{2,6},{3,7},{4,0},{5,1},{6,2},{7,3},{8,12},{9,13},{10,... | collective-permute-start | bytes 786440 | tf_op jit(solution)/shard_map/ppermute | solution.py:166
  238.7 10.3 %collective-permute-start.8 = (bf16[1024,128]{1,0:T(8,128)(2,1)S(1)}, bf16[1024,128]{1,0:T(8,128)(2,1)S(1)}, u32[]{:S(2)}, u32[]{:S(2)}) collective-permute-start(bf16[1024,128]{1,0:T(8,128)(2,1)S(1)} %get-tuple-element.25), channel_id=1, source_target_pairs={{2,4},{3,5},{6,0},{7,1},{10,12},{11,13},{14,8},{15,9},{18,20},{19,... | collective-permute-start | bytes 786440 | tf_op jit(solution)/shard_map/ppermute | solution.py:166
  240.0 19.8 %collective-permute-start.7 = (bf16[1024,128]{1,0:T(8,128)(2,1)S(1)}, bf16[1024,128]{1,0:T(8,128)(2,1)S(1)}, u32[]{:S(2)}, u32[]{:S(2)}) collective-permute-start(bf16[1024,128]{1,0:T(8,128)(2,1)S(1)} %get-tuple-element.26), channel_id=1, source_target_pairs={{1,4},{2,5},{3,6},{5,0},{6,1},{7,2},{9,12},{10,13},{11,14},{13,8},... | collective-permute-start | bytes 786440 | tf_op jit(solution)/shard_map/ppermute | solution.py:166
  241.3 43.6 %collective-permute-start.4 = (bf16[1024,1024]{1,0:T(8,128)(2,1)}, bf16[1024,1024]{1,0:T(8,128)(2,1)}, u32[]{:S(2)}, u32[]{:S(2)}) collective-permute-start(bf16[1024,1024]{1,0:T(8,128)(2,1)} %copy-done.3), channel_id=1, source_target_pairs={{0,4},{1,5},{2,6},{3,7},{4,0},{5,1},{6,2},{7,3},{8,12},{9,13},{10,... | collective-permute-start | bytes 6291464 | tf_op jit(solution)/shard_map/ppermute | solution.py:166
  242.8 42.6 %collective-permute-start.5 = (bf16[1024,1024]{1,0:T(8,128)(2,1)}, bf16[1024,1024]{1,0:T(8,128)(2,1)}, u32[]{:S(2)}, u32[]{:S(2)}) collective-permute-start(bf16[1024,1024]{1,0:T(8,128)(2,1)} %copy-done.2), channel_id=1, source_target_pairs={{0,4},{1,5},{2,6},{3,7},{4,0},{5,1},{6,2},{7,3},{8,12},{9,13},{10,... | collective-permute-start | bytes 6291464 | tf_op jit(solution)/shard_map/ppermute | solution.py:166
  260.7 12.4 %copy-start.18 = (bf16[1024,512]{1,0:T(8,128)(2,1)S(1)}, bf16[1024,512]{1,0:T(8,128)(2,1)}, u32[]{:S(2)}) copy-start(bf16[1024,512]{1,0:T(8,128)(2,1)} %all-gather.5.cloned.1.call-done) | copy-start | bytes 3145732
  263.9 23.0 %collective-permute-start.21 = (bf16[512,512]{0,1:T(8,128)(2,1)}, bf16[512,512]{0,1:T(8,128)(2,1)S(1)}, u32[]{:S(2)}, u32[]{:S(2)}) collective-permute-start(bf16[512,512]{0,1:T(8,128)(2,1)} %convolution_convert_fusion.2), channel_id=1, source_target_pairs={{0,1},{1,2},{2,3},{3,0},{4,5},{5,6},{6,7},{7,4},{8,9},{9,10},{10,1... | collective-permute-start | bytes 1572872 | tf_op jit(solution)/shard_map/ppermute | solution.py:208
  273.1 21.1 %collective-permute-start.22 = (bf16[512,512]{0,1:T(8,128)(2,1)S(1)}, bf16[512,512]{0,1:T(8,128)(2,1)S(1)}, u32[]{:S(2)}, u32[]{:S(2)}) collective-permute-start(bf16[512,512]{0,1:T(8,128)(2,1)S(1)} %convolution_convert_fusion.1), channel_id=1, source_target_pairs={{0,2},{1,3},{2,0},{3,1},{4,6},{5,7},{6,4},{7,5},{8,10},{9,11},{10,... | collective-permute-start | bytes 1572872 | tf_op jit(solution)/shard_map/ppermute | solution.py:208
  276.0 19.0 %collective-permute-start.23 = (bf16[512,512]{0,1:T(8,128)(2,1)}, bf16[512,512]{0,1:T(8,128)(2,1)S(1)}, u32[]{:S(2)}, u32[]{:S(2)}) collective-permute-start(bf16[512,512]{0,1:T(8,128)(2,1)} %convolution_convert_fusion), channel_id=1, source_target_pairs={{0,3},{1,0},{2,1},{3,2},{4,7},{5,4},{6,5},{7,6},{8,11},{9,8},{10,9... | collective-permute-start | bytes 1572872 | tf_op jit(solution)/shard_map/ppermute | solution.py:208
  279.4 4.8 %copy-start.17 = (bf16[1,1024,2048]{2,1,0:T(8,128)(2,1)S(1)}, bf16[1,1024,2048]{2,1,0:T(8,128)(2,1)}, u32[]{:S(2)}) copy-start(bf16[1,1024,2048]{2,1,0:T(8,128)(2,1)} %param.9) | copy-start | bytes 12582916
  279.4 4.8 %copy-start.19 = (bf16[1024,512]{1,0:T(8,128)(2,1)S(1)}, bf16[1024,512]{1,0:T(8,128)(2,1)}, u32[]{:S(2)}) copy-start(bf16[1024,512]{1,0:T(8,128)(2,1)} %all-gather.3.cloned.1.call-done) | copy-start | bytes 3145732
  284.9 20.8 %collective-permute-start.18 = (bf16[512,512]{0,1:T(8,128)(2,1)S(1)}, bf16[512,512]{0,1:T(8,128)(2,1)S(1)}, u32[]{:S(2)}, u32[]{:S(2)}) collective-permute-start(bf16[512,512]{0,1:T(8,128)(2,1)S(1)} %convolution_convert_fusion.5), channel_id=1, source_target_pairs={{0,1},{1,2},{2,3},{3,0},{4,5},{5,6},{6,7},{7,4},{8,9},{9,10},{10,1... | collective-permute-start | bytes 1572872 | tf_op jit(solution)/shard_map/ppermute | solution.py:208
  285.5 30.7 %collective-permute-start.19 = (bf16[512,512]{0,1:T(8,128)(2,1)S(1)}, bf16[512,512]{0,1:T(8,128)(2,1)S(1)}, u32[]{:S(2)}, u32[]{:S(2)}) collective-permute-start(bf16[512,512]{0,1:T(8,128)(2,1)S(1)} %convolution_convert_fusion.4), channel_id=1, source_target_pairs={{0,2},{1,3},{2,0},{3,1},{4,6},{5,7},{6,4},{7,5},{8,10},{9,11},{10,... | collective-permute-start | bytes 1572872 | tf_op jit(solution)/shard_map/ppermute | solution.py:208
  286.9 30.4 %collective-permute-start.20 = (bf16[512,512]{0,1:T(8,128)(2,1)S(1)}, bf16[512,512]{0,1:T(8,128)(2,1)S(1)}, u32[]{:S(2)}, u32[]{:S(2)}) collective-permute-start(bf16[512,512]{0,1:T(8,128)(2,1)S(1)} %convolution_convert_fusion.3), channel_id=1, source_target_pairs={{0,3},{1,0},{2,1},{3,2},{4,7},{5,4},{6,5},{7,6},{8,11},{9,8},{10,9... | collective-permute-start | bytes 1572872 | tf_op jit(solution)/shard_map/ppermute | solution.py:208
  (14 other events, 19.4 us)
Sparse Core Ops, SparseCore 0:
  141.3 33.4 all-gather.4
  238.2 41.1 all-gather.2
